TPU v7x, 32 devices: a whole 2x2x4 slice. The times are simulated.
32 devices in a mesh: grp: 2 (over x), rows: 16 (over z, y, core).
Axes of the slice: x: 2, y: 2, z: 4, core: 2. Of those that a mesh axis runs over, the one named last changes fastest.
Arguments:
- histories: float32 [4096, 384], P(('grp', 'rows')), parts along dimension 0, may hold values from -6 to 6
- modal_map: float32 [4096, 8192], P(('grp', 'rows')), parts along dimension 0, may hold values from -0.1875 to 0.1875
- recovery: float32 [8192, 8192], P(('grp', 'rows')), parts along dimension 0, may hold values from -0.0625 to 0.0625
Outputs:
- responses: float32 [8192, 384], P(('grp', 'rows')), parts along dimension 0
- peak_response: float32 [4, 8192], P(None, ('grp', 'rows')), parts along dimension 1
- rms_response: float32 [4, 8192], P(None, ('grp', 'rows')), parts along dimension 1
There are 2 independent parts, one for each index of `grp`. A program takes and returns all parts, laid end to end along the dimension named above; each array names one. Nothing has to cross between parts.
All inputs are finite; a program needn't handle non-finite values.
Results may differ from a plain program's by a relative error of at most 0.000071.
Values sent between devices are 32-bit elements; how exact they have to be, the bound alone decides.
A program may use at most 64 MiB of HBM per device.

v0:
```python
import jax
import jax.numpy as jnp
from jax import lax
from jax.sharding import PartitionSpec as P

CASES = 4
epsilon = 1e-06


def shards(histories, modal_map, recovery):
    time_cols = histories.shape[1]
    modal_rows = lax.psum_scatter(
        lax.dot_general(
            modal_map,
            histories,
            (((0,), (0,)), ((), ())),
            precision=lax.Precision.HIGHEST,
            preferred_element_type=jnp.float32,
        ),
        "rows",
        scatter_dimension=0,
        tiled=True,
    )
    responses = jnp.dot(
        recovery,
        lax.all_gather(modal_rows, "rows", axis=0, tiled=True),
        precision=lax.Precision.HIGHEST,
        preferred_element_type=jnp.float32,
    )
    by_case = responses.reshape(responses.shape[0], CASES, time_cols // CASES)
    peak_response = jnp.max(jnp.abs(by_case), axis=2).T
    rms_response = jnp.sqrt(jnp.mean(by_case * by_case, axis=2) + epsilon).T
    return (responses, peak_response, rms_response)


def solution(mesh):
    return jax.shard_map(
        shards,
        mesh=mesh,
        in_specs=(P(("grp", "rows"), None), P(("grp", "rows"), None), P(("grp", "rows"), None)),
        out_specs=(P(("grp", "rows"), None), P(None, ("grp", "rows")), P(None, ("grp", "rows"))),
        check_vma=False,
    )
```

profile of v0, /device:TPU:0, one launch (start us, length us, event | category | flops | bytes accessed | tf_op | source)
XLA Modules:
  0.0 294.4 jit_solution(7221013684479145059)
XLA Ops:
  7.2 0.0 copy-start
  7.2 0.0 reduce-scatter.2.cloned.1.call-start
  7.2 0.9 copy-done
  8.1 13.6 %fusion.1 = f32[8192,384]{1,0:T(8,128)} fusion(f32[128,8192]{1,0:T(8,128)} %param.4, f32[128,384]{1,0:T(8,128)S(1)} %copy-done), kind=kOutput, calls=%fused_computation.3 | convolution fusion | flops 4831838208 | bytes 16973824 | tf_op jit(solution)/shard_map/dot_general | solution.py:13
  21.7 0.0 reduce-scatter.2.cloned.1.call-update
  21.7 0.2 all-gather.2.cloned.1.call-start
  21.9 137.2 %reduce-scatter.2.cloned.1.call-done = f32[512,384]{1,0:T(8,128)} async-done(((f32[8192,384]{1,0:T(8,128)}), f32[512,384]{1,0:T(8,128)}) %reduce-scatter.2.cloned.1.call-update) | async-done | bytes 786448 | tf_op jit(solution)/shard_map/reduce_scatter | solution.py:12
  159.2 0.0 all-gather.2.cloned.1.call-update
  159.2 102.2 %all-gather.2.cloned.1.call-done = f32[8192,384]{1,0:T(8,128)} async-done(((f32[512,384]{1,0:T(8,128)}), f32[8192,384]{1,0:T(8,128)}) %all-gather.2.cloned.1.call-update) | async-done | bytes 12582928 | tf_op jit(solution)/shard_map/all_gather | solution.py:26
  261.4 23.9 %fusion = (f32[256,384]{0,1:T(8,128)S(1)}, f32[256,384]{0,1:T(8,128)S(1)}, f32[256,384]{0,1:T(8,128)S(1)}) fusion(f32[8192,384]{1,0:T(8,128)} %all-gather.2.cloned.1.call-done, f32[256,8192]{1,0:T(8,128)} %param.5), kind=kOutput, calls=%fused_computation.2 | convolution fusion | flops 9663873024 | bytes 22151168 | tf_op jit(solution)/shard_map/dot_general | solution.py:24
  285.4 0.6 sqrt_bitcast_fusion
  286.0 0.9 copy.6
  286.9 0.6 reduce_max.9
  (1 shorter events, 0.0 us)
Async XLA Ops:
  7.2 0.9 copy-start
  7.2 152.0 %reduce-scatter.2.cloned.1.call-start = ((), (), s32[]{:S(2)}) async-start(), calls=%async_computation.1 | async-start | bytes 13369344 | tf_op jit(solution)/shard_map/reduce_scatter | solution.py:12
  21.7 239.7 %all-gather.2.cloned.1.call-start = ((), (), s32[]{:S(2)}) async-start(), calls=%async_computation.2 | async-start | bytes 13369344 | tf_op jit(solution)/shard_map/all_gather | solution.py:26
Sparse Core Ops, SparseCore 0:
  21.8 137.3 reduce-scatter.1
  161.5 99.8 all-gather.1
where the time goes:
time: 295 us; the launch traced here: 294 us
  waiting for transfers between devices  239 us (81%)
  matrix products  37.5 us (13%)
  between operations  14.1 us (5%)
    reduce_scatter x1, waiting for transfers between devices, shards(): lax.psum_scatter(lax.dot_general(modal_map, histories, (((0,), (0,)), (()...  137 us
    all_gather x1, waiting for transfers between devices, shards(): lax.all_gather(modal_rows, 'rows', axis=0, tiled=True)  102 us
    dot_general x1, matrix products, shards(): jnp.dot(recovery, lax.all_gather(modal_rows, 'rows', axis=0, tiled=True),...  23.9 us
    dot_general x1, matrix products, shards(): lax.dot_general(modal_map, histories, (((0,), (0,)), ((), ())), precision...  13.6 us
  transfers between devices with their start and end apart: 2, of which 2 were waited for; matrix products, arithmetic and copies ran while one was open for 0% of the time, Pallas kernels for 0%

commit v1 on v0

--- a/solution.py
+++ b/solution.py
@@ -5,6 +5,19 @@
 
 CASES = 4
 epsilon = 1e-06
+
+
+def collect(value, axis, dim):
+    ways = lax.axis_size(axis)
+    up = [(d, (d + 1) % ways) for d in range(ways)]
+    down = [(d, (d - 1) % ways) for d in range(ways)]
+    earlier, later = ([value], [value])
+    for _ in range(ways // 2):
+        earlier.append(lax.ppermute(earlier[-1], axis, up))
+    for _ in range((ways - 1) // 2):
+        later.append(lax.ppermute(later[-1], axis, down))
+    line = jnp.concatenate([*earlier[::-1], *later[1:]], axis=dim)
+    return jnp.roll(line, (lax.axis_index(axis) - ways // 2) * value.shape[dim], axis=dim)
 
 
 def shards(histories, modal_map, recovery):
@@ -23,7 +36,7 @@
     )
     responses = jnp.dot(
         recovery,
-        lax.all_gather(modal_rows, "rows", axis=0, tiled=True),
+        collect(modal_rows, "rows", 0),
         precision=lax.Precision.HIGHEST,
         preferred_element_type=jnp.float32,
     )

time: 295 us -> 386 us (1.31); the launches traced: 294 us -> 380 us
  starting transfers between devices: 0.26 us -> 77.4 us
  local copies, waits for them, and re-layouts: 1.79 us -> 53.2 us
  waiting for transfers between devices: 239 us -> 197 us
    all_gather x1 -> x0, waiting for transfers between devices: 102 us -> none  [shards(): lax.all_gather(modal_rows, 'rows', axis=0, tiled=True)]
    ppermute x0 -> x15, starting transfers between devices: none -> 77.3 us  [the longest x8 65.4 us: collect(): earlier.append(lax.ppermute(earlier[-1], axis, up))]
    ppermute x0 -> x15, waiting for transfers between devices: none -> 59.3 us  [the longest x8 59.3 us: collect(): earlier.append(lax.ppermute(earlier[-1], axis, up))]
    unnamed x3 -> x68, local copies, waits for them, and re-layouts: 1.79 us -> 52.2 us
  transfers between devices with their start and end apart: 2 -> 16, of which waited for: 2 -> 9; matrix products, arithmetic and copies ran while one was open for 0% -> 7% of each run, Pallas kernels for 0% -> 0%
where the time goes in v1:
time: 386 us; the launch traced here: 380 us
  waiting for transfers between devices  197 us (51%)
  starting transfers between devices  77.4 us (20%)
  local copies, waits for them, and re-layouts  53.2 us (14%)
  matrix products  36.7 us (10%)
  between operations  14.2 us (4%)
    reduce_scatter x1, waiting for transfers between devices, shards(): lax.psum_scatter(lax.dot_general(modal_map, histories, (((0,), (0,)), (()...  137 us
    ppermute x8, starting transfers between devices, collect(): earlier.append(lax.ppermute(earlier[-1], axis, up))  65.4 us
    ppermute x8, waiting for transfers between devices, collect(): earlier.append(lax.ppermute(earlier[-1], axis, up))  59.3 us
    unnamed x68, local copies, waits for them, and re-layouts  52.2 us
    dot_general x1, matrix products, shards(): jnp.dot(recovery, collect(modal_rows, 'rows', 0), precision=lax.Precision...  23 us
    dot_general x1, matrix products, shards(): lax.dot_general(modal_map, histories, (((0,), (0,)), ((), ())), precision...  13.6 us
    ppermute x7, starting transfers between devices, collect(): later.append(lax.ppermute(later[-1], axis, down))  12 us
  transfers between devices with their start and end apart: 16, of which 9 were waited for; matrix products, arithmetic and copies ran while one was open for 7% of the time, Pallas kernels for 0%

profile of v1, /device:TPU:0, one launch (start us, length us, event | category | flops | bytes accessed | tf_op | source)
XLA Modules:
  0.0 379.5 jit_solution(10744597759922514286)
XLA Ops:
  8.1 13.6 %fusion.7 = f32[8192,384]{1,0:T(8,128)} fusion(f32[128,8192]{1,0:T(8,128)} %param.4, f32[128,384]{1,0:T(8,128)S(1)} %copy-done), kind=kOutput, calls=%fused_computation.38 | convolution fusion | flops 4831838208 | bytes 16973824 | tf_op jit(solution)/shard_map/dot_general | solution.py:26
  21.8 137.5 %reduce-scatter.2.cloned.1.call-done = f32[512,384]{1,0:T(8,128)} async-done(((f32[8192,384]{1,0:T(8,128)}), f32[512,384]{1,0:T(8,128)}) %reduce-scatter.2.cloned.1.call-update) | async-done | bytes 786448 | tf_op jit(solution)/shard_map/reduce_scatter | solution.py:25
  159.2 14.3 %collective-permute-done = f32[512,384]{1,0:T(8,128)S(1)} collective-permute-done((f32[512,384]{1,0:T(8,128)}, f32[512,384]{1,0:T(8,128)S(1)}, u32[]{:S(2)}, u32[]{:S(2)}) %collective-permute-start) | collective-permute-done | bytes 786464 | tf_op jit(solution)/shard_map/ppermute | solution.py:16
  173.6 4.4 %collective-permute-start.8 = (f32[512,384]{1,0:T(8,128)}, f32[512,384]{1,0:T(8,128)S(1)}, u32[]{:S(2)}, u32[]{:S(2)}) collective-permute-start(f32[512,384]{1,0:T(8,128)} %reduce-scatter.2.cloned.1.call-done), channel_id=1, source_target_pairs={{0,15},{1,0},{2,1},{3,2},{4,3},{5,4},{6,5},{7,6},{8,7},{9,8},{10,9... | collective-permute-start | bytes 2359304 | tf_op jit(solution)/shard_map/ppermute | solution.py:18
  178.0 9.8 %collective-permute-done.1 = f32[512,384]{1,0:T(8,128)S(1)} collective-permute-done((f32[512,384]{1,0:T(8,128)S(1)}, f32[512,384]{1,0:T(8,128)S(1)}, u32[]{:S(2)}, u32[]{:S(2)}) %collective-permute-start.1) | collective-permute-done | bytes 786464 | tf_op jit(solution)/shard_map/ppermute | solution.py:16
  189.8 2.6 collective-permute-start.9
  192.4 9.6 %collective-permute-done.2 = f32[512,384]{1,0:T(8,128)S(1)} collective-permute-done((f32[512,384]{1,0:T(8,128)S(1)}, f32[512,384]{1,0:T(8,128)S(1)}, u32[]{:S(2)}, u32[]{:S(2)}) %collective-permute-start.2) | collective-permute-done | bytes 786464 | tf_op jit(solution)/shard_map/ppermute | solution.py:16
  202.0 6.0 %collective-permute-start.3 = (f32[512,384]{1,0:T(8,128)S(1)}, f32[512,384]{1,0:T(8,128)S(1)}, u32[]{:S(2)}, u32[]{:S(2)}) collective-permute-start(f32[512,384]{1,0:T(8,128)S(1)} %collective-permute-done.2), channel_id=1, source_target_pairs={{0,1},{1,2},{2,3},{3,4},{4,5},{5,6},{6,7},{7,8},{8,9},{9,10},{10,1... | collective-permute-start | bytes 2359304 | tf_op jit(solution)/shard_map/ppermute | solution.py:16
  208.9 7.3 %collective-permute-done.3 = f32[512,384]{1,0:T(8,128)S(1)} collective-permute-done((f32[512,384]{1,0:T(8,128)S(1)}, f32[512,384]{1,0:T(8,128)S(1)}, u32[]{:S(2)}, u32[]{:S(2)}) %collective-permute-start.3) | collective-permute-done | bytes 786464 | tf_op jit(solution)/shard_map/ppermute | solution.py:16
  216.2 11.7 %collective-permute-start.4 = (f32[512,384]{1,0:T(8,128)S(1)}, f32[512,384]{1,0:T(8,128)S(1)}, u32[]{:S(2)}, u32[]{:S(2)}) collective-permute-start(f32[512,384]{1,0:T(8,128)S(1)} %collective-permute-done.3), channel_id=1, source_target_pairs={{0,1},{1,2},{2,3},{3,4},{4,5},{5,6},{6,7},{7,8},{8,9},{9,10},{10,1... | collective-permute-start | bytes 2359304 | tf_op jit(solution)/shard_map/ppermute | solution.py:16
  228.8 3.3 collective-permute-done.4
  232.1 15.6 %collective-permute-start.5 = (f32[512,384]{1,0:T(8,128)S(1)}, f32[512,384]{1,0:T(8,128)S(1)}, u32[]{:S(2)}, u32[]{:S(2)}) collective-permute-start(f32[512,384]{1,0:T(8,128)S(1)} %collective-permute-done.4), channel_id=1, source_target_pairs={{0,1},{1,2},{2,3},{3,4},{4,5},{5,6},{6,7},{7,8},{8,9},{9,10},{10,1... | collective-permute-start | bytes 2359304 | tf_op jit(solution)/shard_map/ppermute | solution.py:16
  248.6 2.2 collective-permute-done.5
  250.8 15.8 %collective-permute-start.6 = (f32[512,384]{1,0:T(8,128)S(1)}, f32[512,384]{1,0:T(8,128)}, u32[]{:S(2)}, u32[]{:S(2)}) collective-permute-start(f32[512,384]{1,0:T(8,128)S(1)} %collective-permute-done.5), channel_id=1, source_target_pairs={{0,1},{1,2},{2,3},{3,4},{4,5},{5,6},{6,7},{7,8},{8,9},{9,10},{10,1... | collective-permute-start | bytes 2359304 | tf_op jit(solution)/shard_map/ppermute | solution.py:16
  266.7 4.9 %collective-permute-done.6 = f32[512,384]{1,0:T(8,128)} collective-permute-done((f32[512,384]{1,0:T(8,128)S(1)}, f32[512,384]{1,0:T(8,128)}, u32[]{:S(2)}, u32[]{:S(2)}) %collective-permute-start.6) | collective-permute-done | bytes 786464 | tf_op jit(solution)/shard_map/ppermute | solution.py:16
  271.6 14.2 %collective-permute-start.7 = (f32[512,384]{1,0:T(8,128)}, f32[512,384]{1,0:T(8,128)}, u32[]{:S(2)}, u32[]{:S(2)}) collective-permute-start(f32[512,384]{1,0:T(8,128)} %collective-permute-done.6), channel_id=1, source_target_pairs={{0,1},{1,2},{2,3},{3,4},{4,5},{5,6},{6,7},{7,8},{8,9},{9,10},{10,1... | collective-permute-start | bytes 2359304 | tf_op jit(solution)/shard_map/ppermute | solution.py:16
  285.9 4.8 %collective-permute-start.14 = (f32[512,384]{1,0:T(8,128)}, f32[512,384]{1,0:T(8,128)S(1)}, u32[]{:S(2)}, u32[]{:S(2)}) collective-permute-start(f32[512,384]{1,0:T(8,128)} %collective-permute-done.13), channel_id=1, source_target_pairs={{0,15},{1,0},{2,1},{3,2},{4,3},{5,4},{6,5},{7,6},{8,7},{9,8},{10,9... | collective-permute-start | bytes 2359304 | tf_op jit(solution)/shard_map/ppermute | solution.py:18
  290.7 7.9 %collective-permute-done.7 = f32[512,384]{1,0:T(8,128)} collective-permute-done((f32[512,384]{1,0:T(8,128)}, f32[512,384]{1,0:T(8,128)}, u32[]{:S(2)}, u32[]{:S(2)}) %collective-permute-start.7) | collective-permute-done | bytes 786464 | tf_op jit(solution)/shard_map/ppermute | solution.py:16
  298.6 2.1 constant_dynamic-update-slice_fusion.31
  300.7 2.1 constant_dynamic-update-slice_fusion.30
  302.9 2.1 constant_dynamic-update-slice_fusion.29
  307.0 2.1 constant_dynamic-update-slice_fusion.27
  309.1 2.1 constant_dynamic-update-slice_fusion.26
  313.1 2.1 constant_dynamic-update-slice_fusion.23
  316.1 2.1 constant_dynamic-update-slice_fusion.21
  318.2 2.1 constant_dynamic-update-slice_fusion.20
  322.3 2.1 constant_dynamic-update-slice_fusion.18
  324.4 2.1 constant_dynamic-update-slice_fusion.17
  327.4 2.3 constant_dynamic-update-slice_fusion.15
  329.7 2.1 constant_dynamic-update-slice_fusion.14
  342.3 2.1 constant_dynamic-update-slice_fusion.2
  347.4 23.0 %fusion.6 = (f32[256,384]{0,1:T(8,128)S(1)}, f32[256,384]{0,1:T(8,128)S(1)}, f32[256,384]{0,1:T(8,128)S(1)}) fusion(f32[256,8192]{1,0:T(8,128)S(1)} %bitcast.11, f32[16384,384]{1,0:T(8,128)} %constant_dynamic-update-slice_fusion, s32[]{:T(128)S(6)} %select_n.14), kind=kOutput, calls=%fused_computation.37 | convolution fusion | flops 9663873024 | bytes 22151172 | tf_op jit(solution)/shard_map/dot_general | solution.py:37
  (76 shorter events, 29.3 us)
Async XLA Ops:
  7.2 0.9 copy-start
  7.2 152.1 %reduce-scatter.2.cloned.1.call-start = ((), (), s32[]{:S(2)}) async-start(), calls=%async_computation.1 | async-start | bytes 13369344 | tf_op jit(solution)/shard_map/reduce_scatter | solution.py:25
  159.2 178.3 %copy-start.1 = (f32[512,384]{1,0:T(8,128)S(1)}, f32[512,384]{1,0:T(8,128)}, u32[]{:S(2)}) copy-start(f32[512,384]{1,0:T(8,128)} %reduce-scatter.2.cloned.1.call-done) | copy-start | bytes 2359300
  159.2 14.3 %collective-permute-start = (f32[512,384]{1,0:T(8,128)}, f32[512,384]{1,0:T(8,128)S(1)}, u32[]{:S(2)}, u32[]{:S(2)}) collective-permute-start(f32[512,384]{1,0:T(8,128)} %reduce-scatter.2.cloned.1.call-done), channel_id=1, source_target_pairs={{0,1},{1,2},{2,3},{3,4},{4,5},{5,6},{6,7},{7,8},{8,9},{9,10},{10,1... | collective-permute-start | bytes 2359304 | tf_op jit(solution)/shard_map/ppermute | solution.py:16
  173.6 14.2 %collective-permute-start.1 = (f32[512,384]{1,0:T(8,128)S(1)}, f32[512,384]{1,0:T(8,128)S(1)}, u32[]{:S(2)}, u32[]{:S(2)}) collective-permute-start(f32[512,384]{1,0:T(8,128)S(1)} %collective-permute-done), channel_id=1, source_target_pairs={{0,1},{1,2},{2,3},{3,4},{4,5},{5,6},{6,7},{7,8},{8,9},{9,10},{10,1... | collective-permute-start | bytes 2359304 | tf_op jit(solution)/shard_map/ppermute | solution.py:16
  173.6 16.2 %collective-permute-start.8 = (f32[512,384]{1,0:T(8,128)}, f32[512,384]{1,0:T(8,128)S(1)}, u32[]{:S(2)}, u32[]{:S(2)}) collective-permute-start(f32[512,384]{1,0:T(8,128)} %reduce-scatter.2.cloned.1.call-done), channel_id=1, source_target_pairs={{0,15},{1,0},{2,1},{3,2},{4,3},{5,4},{6,5},{7,6},{8,7},{9,8},{10,9... | collective-permute-start | bytes 2359304 | tf_op jit(solution)/shard_map/ppermute | solution.py:18
  187.8 14.2 %collective-permute-start.2 = (f32[512,384]{1,0:T(8,128)S(1)}, f32[512,384]{1,0:T(8,128)S(1)}, u32[]{:S(2)}, u32[]{:S(2)}) collective-permute-start(f32[512,384]{1,0:T(8,128)S(1)} %collective-permute-done.1), channel_id=1, source_target_pairs={{0,1},{1,2},{2,3},{3,4},{4,5},{5,6},{6,7},{7,8},{8,9},{9,10},{10,1... | collective-permute-start | bytes 2359304 | tf_op jit(solution)/shard_map/ppermute | solution.py:16
  189.8 18.2 %collective-permute-start.9 = (f32[512,384]{1,0:T(8,128)S(1)}, f32[512,384]{1,0:T(8,128)S(1)}, u32[]{:S(2)}, u32[]{:S(2)}) collective-permute-start(f32[512,384]{1,0:T(8,128)S(1)} %collective-permute-done.8), channel_id=1, source_target_pairs={{0,15},{1,0},{2,1},{3,2},{4,3},{5,4},{6,5},{7,6},{8,7},{9,8},{10,9... | collective-permute-start | bytes 2359304 | tf_op jit(solution)/shard_map/ppermute | solution.py:18
  202.0 25.9 %copy-start.4 = (f32[512,384]{1,0:T(8,128)}, f32[512,384]{1,0:T(8,128)S(1)}, u32[]{:S(2)}) copy-start(f32[512,384]{1,0:T(8,128)S(1)} %collective-permute-done.2) | copy-start | bytes 2359300
  202.0 14.2 %collective-permute-start.3 = (f32[512,384]{1,0:T(8,128)S(1)}, f32[512,384]{1,0:T(8,128)S(1)}, u32[]{:S(2)}, u32[]{:S(2)}) collective-permute-start(f32[512,384]{1,0:T(8,128)S(1)} %collective-permute-done.2), channel_id=1, source_target_pairs={{0,1},{1,2},{2,3},{3,4},{4,5},{5,6},{6,7},{7,8},{8,9},{9,10},{10,1... | collective-permute-start | bytes 2359304 | tf_op jit(solution)/shard_map/ppermute | solution.py:16
  208.0 0.9 copy-start.2
  208.9 18.9 %collective-permute-start.10 = (f32[512,384]{1,0:T(8,128)S(1)}, f32[512,384]{1,0:T(8,128)S(1)}, u32[]{:S(2)}, u32[]{:S(2)}) collective-permute-start(f32[512,384]{1,0:T(8,128)S(1)} %collective-permute-done.9), channel_id=1, source_target_pairs={{0,15},{1,0},{2,1},{3,2},{4,3},{5,4},{6,5},{7,6},{8,7},{9,8},{10,9... | collective-permute-start | bytes 2359304 | tf_op jit(solution)/shard_map/ppermute | solution.py:18
  216.2 50.5 %copy-start.10 = (f32[512,384]{1,0:T(8,128)}, f32[512,384]{1,0:T(8,128)S(1)}, u32[]{:S(2)}) copy-start(f32[512,384]{1,0:T(8,128)S(1)} %collective-permute-done.3) | copy-start | bytes 2359300
  216.2 15.9 %collective-permute-start.4 = (f32[512,384]{1,0:T(8,128)S(1)}, f32[512,384]{1,0:T(8,128)S(1)}, u32[]{:S(2)}, u32[]{:S(2)}) collective-permute-start(f32[512,384]{1,0:T(8,128)S(1)} %collective-permute-done.3), channel_id=1, source_target_pairs={{0,1},{1,2},{2,3},{3,4},{4,5},{5,6},{6,7},{7,8},{8,9},{9,10},{10,1... | collective-permute-start | bytes 2359304 | tf_op jit(solution)/shard_map/ppermute | solution.py:16
  227.9 19.8 %collective-permute-start.11 = (f32[512,384]{1,0:T(8,128)S(1)}, f32[512,384]{1,0:T(8,128)S(1)}, u32[]{:S(2)}, u32[]{:S(2)}) collective-permute-start(f32[512,384]{1,0:T(8,128)S(1)} %collective-permute-done.10), channel_id=1, source_target_pairs={{0,15},{1,0},{2,1},{3,2},{4,3},{5,4},{6,5},{7,6},{8,7},{9,8},{10,9... | collective-permute-start | bytes 2359304 | tf_op jit(solution)/shard_map/ppermute | solution.py:18
  232.1 34.6 %copy-start.12 = (f32[512,384]{1,0:T(8,128)}, f32[512,384]{1,0:T(8,128)S(1)}, u32[]{:S(2)}) copy-start(f32[512,384]{1,0:T(8,128)S(1)} %collective-permute-done.4) | copy-start | bytes 2359300
  232.1 18.7 %collective-permute-start.5 = (f32[512,384]{1,0:T(8,128)S(1)}, f32[512,384]{1,0:T(8,128)S(1)}, u32[]{:S(2)}, u32[]{:S(2)}) collective-permute-start(f32[512,384]{1,0:T(8,128)S(1)} %collective-permute-done.4), channel_id=1, source_target_pairs={{0,1},{1,2},{2,3},{3,4},{4,5},{5,6},{6,7},{7,8},{8,9},{9,10},{10,1... | collective-permute-start | bytes 2359304 | tf_op jit(solution)/shard_map/ppermute | solution.py:16
  248.6 18.1 %collective-permute-start.12 = (f32[512,384]{1,0:T(8,128)S(1)}, f32[512,384]{1,0:T(8,128)}, u32[]{:S(2)}, u32[]{:S(2)}) collective-permute-start(f32[512,384]{1,0:T(8,128)S(1)} %collective-permute-done.11), channel_id=1, source_target_pairs={{0,15},{1,0},{2,1},{3,2},{4,3},{5,4},{6,5},{7,6},{8,7},{9,8},{10,9... | collective-permute-start | bytes 2359304 | tf_op jit(solution)/shard_map/ppermute | solution.py:18
  250.8 20.8 %copy-start.14 = (f32[512,384]{1,0:T(8,128)}, f32[512,384]{1,0:T(8,128)S(1)}, u32[]{:S(2)}) copy-start(f32[512,384]{1,0:T(8,128)S(1)} %collective-permute-done.5) | copy-start | bytes 2359300
  250.8 20.8 %collective-permute-start.6 = (f32[512,384]{1,0:T(8,128)S(1)}, f32[512,384]{1,0:T(8,128)}, u32[]{:S(2)}, u32[]{:S(2)}) collective-permute-start(f32[512,384]{1,0:T(8,128)S(1)} %collective-permute-done.5), channel_id=1, source_target_pairs={{0,1},{1,2},{2,3},{3,4},{4,5},{5,6},{6,7},{7,8},{8,9},{9,10},{10,1... | collective-permute-start | bytes 2359304 | tf_op jit(solution)/shard_map/ppermute | solution.py:16
  266.7 19.2 %collective-permute-start.13 = (f32[512,384]{1,0:T(8,128)}, f32[512,384]{1,0:T(8,128)}, u32[]{:S(2)}, u32[]{:S(2)}) collective-permute-start(f32[512,384]{1,0:T(8,128)} %collective-permute-done.12), channel_id=1, source_target_pairs={{0,15},{1,0},{2,1},{3,2},{4,3},{5,4},{6,5},{7,6},{8,7},{9,8},{10,9... | collective-permute-start | bytes 2359304 | tf_op jit(solution)/shard_map/ppermute | solution.py:18
  271.6 27.0 %collective-permute-start.7 = (f32[512,384]{1,0:T(8,128)}, f32[512,384]{1,0:T(8,128)}, u32[]{:S(2)}, u32[]{:S(2)}) collective-permute-start(f32[512,384]{1,0:T(8,128)} %collective-permute-done.6), channel_id=1, source_target_pairs={{0,1},{1,2},{2,3},{3,4},{4,5},{5,6},{6,7},{7,8},{8,9},{9,10},{10,1... | collective-permute-start | bytes 2359304 | tf_op jit(solution)/shard_map/ppermute | solution.py:16
  285.8 46.0 %copy-start.15 = (f32[512,384]{1,0:T(8,128)S(1)}, f32[512,384]{1,0:T(8,128)}, u32[]{:S(2)}) copy-start(f32[512,384]{1,0:T(8,128)} %copy-done.14) | copy-start | bytes 2359300
  285.8 46.9 %copy-start.13 = (f32[512,384]{1,0:T(8,128)S(1)}, f32[512,384]{1,0:T(8,128)}, u32[]{:S(2)}) copy-start(f32[512,384]{1,0:T(8,128)} %copy-done.12) | copy-start | bytes 2359300
  285.8 47.9 %copy-start.11 = (f32[512,384]{1,0:T(8,128)S(1)}, f32[512,384]{1,0:T(8,128)}, u32[]{:S(2)}) copy-start(f32[512,384]{1,0:T(8,128)} %copy-done.10) | copy-start | bytes 2359300
  285.8 48.8 %copy-start.5 = (f32[512,384]{1,0:T(8,128)S(1)}, f32[512,384]{1,0:T(8,128)}, u32[]{:S(2)}) copy-start(f32[512,384]{1,0:T(8,128)} %copy-done.4) | copy-start | bytes 2359300
  285.8 53.6 %copy-start.3 = (f32[512,384]{1,0:T(8,128)S(1)}, f32[512,384]{1,0:T(8,128)}, u32[]{:S(2)}) copy-start(f32[512,384]{1,0:T(8,128)} %copy-done.2) | copy-start | bytes 2359300
  285.9 54.5 %copy-start.7 = (f32[512,384]{1,0:T(8,128)S(1)}, f32[512,384]{1,0:T(8,128)}, u32[]{:S(2)}) copy-start(f32[512,384]{1,0:T(8,128)} %copy-done.6) | copy-start | bytes 2359300
  285.9 55.5 %copy-start.9 = (f32[512,384]{1,0:T(8,128)S(1)}, f32[512,384]{1,0:T(8,128)}, u32[]{:S(2)}) copy-start(f32[512,384]{1,0:T(8,128)} %copy-done.8) | copy-start | bytes 2359300
  285.9 61.6 %slice-start = ((s8[8388608]{0:T(1024)(128)(4,1)}), s8[4194304]{0:T(1024)(128)(4,1)S(1)}, s32[]{:S(2)}) async-start(s8[8388608]{0:T(1024)(128)(4,1)} %bitcast.10), calls=%async_computation.2 | async-start | bytes 8388608
  285.9 40.6 %collective-permute-start.14 = (f32[512,384]{1,0:T(8,128)}, f32[512,384]{1,0:T(8,128)S(1)}, u32[]{:S(2)}, u32[]{:S(2)}) collective-permute-start(f32[512,384]{1,0:T(8,128)} %collective-permute-done.13), channel_id=1, source_target_pairs={{0,15},{1,0},{2,1},{3,2},{4,3},{5,4},{6,5},{7,6},{8,7},{9,8},{10,9... | collective-permute-start | bytes 2359304 | tf_op jit(solution)/shard_map/ppermute | solution.py:18
  327.4 20.0 %slice-start.1 = ((s8[8388608]{0:T(1024)(128)(4,1)}), s8[4194304]{0:T(1024)(128)(4,1)S(1)}, s32[]{:S(2)}) async-start(s8[8388608]{0:T(1024)(128)(4,1)} %bitcast.10), calls=%async_computation.3 | async-start | bytes 8388608
  (2 other events, 1.8 us)
Sparse Core Ops, SparseCore 0:
  21.9 137.3 reduce-scatter.1
